TPU v7x, 512 devices: a whole 4x8x8 slice. The times are simulated.
512 devices in a mesh: grow: 32 (over x_hi, y, core), gcol: 16 (over z, x_lo).
Axes of the slice: x: 4 (x_hi: 2, x_lo: 2; x = x_hi * 2 + x_lo), y: 8, z: 8, core: 2. Of those that a mesh axis runs over, the one named last changes fastest.
Arguments:
- coefficients: bfloat16 [20480, 49152], P('grow', 'gcol'), may hold values from -0.02734375 to 0.02734375
- tile_mask: int32 [160, 384], P('grow', 'gcol'), may hold values 0 or 1
- duals: float32 [20480], P('grow'), may hold values from -6 to 6
- costs: float32 [49152], P('gcol'), may hold values from -6 to 6
- primal: float32 [49152], P('gcol'), may hold values from 0.1 to 10
- fixed: int32 [49152], P('gcol'), may hold values 0 or 1
Outputs:
- normal_window: float32 [1024, 20480], P('gcol', 'grow')
- factor_window: float32 [1024, 20480], P('gcol', 'grow')
All inputs are finite; a program needn't handle non-finite values. No bound on the sum of `tile_mask` or of `fixed` on one device may be relied on, other than what follows from the above.
Results may differ from a plain program's by a relative error of at most 0.0023.
Values may be sent and summed in bfloat16 or wider, within the bound.
A program may use at most 64 MiB of HBM per device.

v0:
```python
import jax
import jax.numpy as jnp
from jax import lax
from jax.sharding import PartitionSpec as P

PANEL = 512
SOFTNESS = 0.25
DIAGONAL_SHIFT = 0.5


def split_normal(normal, blocks_own, panel_per, rows_dev):
    split = normal.reshape(blocks_own, 2, panel_per, rows_dev)
    own_panel = split[:, 0].reshape(blocks_own * panel_per, rows_dev)
    own_trailing = split[:, 1].reshape(blocks_own * panel_per, rows_dev)
    panel_all = lax.all_gather(own_panel, "gcol", axis=0, tiled=True)
    return (own_trailing, panel_all)


def shards(coefficients, tile_mask, duals, costs, primal, fixed):
    rows_dev, columns = coefficients.shape
    row_count = lax.axis_size("grow")
    col_count = lax.axis_size("gcol")
    panel_per = PANEL // row_count
    blocks_own = row_count // col_count
    local_win = blocks_own * 2 * panel_per
    tile_rows, tile_cols = tile_mask.shape
    side = rows_dev // tile_rows
    expanded = jnp.broadcast_to(
        tile_mask[:, None, :, None], (tile_rows, side, tile_cols, side)
    ).reshape(rows_dev, columns)
    masked = coefficients * expanded.astype(jnp.bfloat16)
    partial_products = jnp.dot(
        duals, masked, preferred_element_type=jnp.float32, precision=lax.Precision.HIGHEST
    )
    products = lax.psum(partial_products, "grow")
    reduced = costs - products
    scaling = (1 - fixed).astype(jnp.float32) * primal / jnp.sqrt(reduced * reduced + SOFTNESS)
    scaled = (masked * scaling[None, :]).astype(jnp.bfloat16)
    window_all = lax.all_gather(masked[: 2 * panel_per], "grow", axis=0, tiled=True)
    col_index = lax.axis_index("gcol")
    normal = lax.psum_scatter(
        lax.dot_general(
            window_all, scaled, (((1,), (1,)), ((), ())), preferred_element_type=jnp.float32
        ),
        "gcol",
        scatter_dimension=0,
        tiled=True,
    )
    own_trailing, panel_all = split_normal(normal, blocks_own, panel_per, rows_dev)
    corner = lax.all_gather(panel_all[:, :panel_per], "grow", axis=1, tiled=True)
    shifted = 0.5 * (corner + corner.T) + DIAGONAL_SHIFT * jnp.eye(PANEL, dtype=jnp.float32)
    lower = jnp.linalg.cholesky(shifted)
    factor_panel = jax.scipy.linalg.solve_triangular(lower, panel_all, lower=True)
    edge_all = lax.all_gather(
        factor_panel[:, panel_per : 2 * panel_per], "grow", axis=1, tiled=True
    )
    own_edge = lax.dynamic_slice_in_dim(
        edge_all, col_index * (blocks_own * panel_per), blocks_own * panel_per, 1
    )
    updated = own_trailing - jnp.dot(own_edge.T, factor_panel, precision=lax.Precision.HIGHEST)
    panel_rows = lax.dynamic_slice_in_dim(
        factor_panel, col_index * (blocks_own * panel_per), blocks_own * panel_per, 0
    )
    factor = jnp.stack(
        [
            panel_rows.reshape(blocks_own, panel_per, rows_dev),
            updated.reshape(blocks_own, panel_per, rows_dev),
        ],
        axis=1,
    )
    return (normal, factor.reshape(local_win, rows_dev))


def solution(mesh):
    placed = (P("grow", "gcol"), P("grow", "gcol"), P("grow"), P("gcol"), P("gcol"), P("gcol"))
    return jax.shard_map(
        shards,
        mesh=mesh,
        in_specs=placed,
        out_specs=(P("gcol", "grow"), P("gcol", "grow")),
        check_vma=False,
    )
```

profile of v0, /device:TPU:1, one launch (start us, length us, event | category | flops | bytes accessed | tf_op | source)
XLA Modules:
  0.0 642.4 jit_solution(5346488050266648543)
XLA Ops:
  9.9 1.9 copy-done
  12.6 3.7 fusion.38
  16.3 130.1 %psum.7 = f32[3072]{0:T(1024)S(1)} all-reduce(f32[3072]{0:T(1024)S(1)} %bitcast.77), channel_id=1, replica_groups=mesh['grow'=32,'gcol'=16] {'grow'}, use_global_device_ids=true, to_apply=%region_0.0 | all-reduce | flops 3072 | bytes 24576 | tf_op jit(solution)/shard_map/psum | solution.py:35
  146.5 9.5 %fusion = f32[1024,640]{1,0:T(8,128)} fusion(bf16[1024,3072]{1,0:T(8,128)(2,1)} %all-gather.5.cloned.1.call-done, bf16[640,3072]{1,0:T(8,128)(2,1)} %copy-done, f32[3072]{0:T(1024)S(1)} %rsqrt_multiply_fusion), kind=kOutput, calls=%fused_computation.3 | convolution fusion | flops 4032430080 | bytes 12857344 | tf_op jit(solution)/shard_map/dot_general | solution.py:42
  156.0 74.2 %reduce-scatter.2.cloned.1.call-done = f32[64,640]{1,0:T(8,128)} async-done(((f32[1024,640]{1,0:T(8,128)}), f32[64,640]{1,0:T(8,128)}) %reduce-scatter.2.cloned.1.call-update) | async-done | bytes 163856 | tf_op jit(solution)/shard_map/reduce_scatter | solution.py:41
  230.3 1.6 fusion.37
  231.9 71.6 %all-gather.7.cloned.1.call-done = f32[512,640]{1,0:T(8,128)} async-done(((f32[32,640]{1,0:T(8,128)}), f32[512,640]{1,0:T(8,128)}) %all-gather.7.cloned.1.call-update) | async-done | bytes 1310736 | tf_op jit(solution)/shard_map/all_gather | solution.py:15
  305.8 94.8 %all-gather.9.cloned.1.call-done = f32[512,512]{0,1:T(8,128)} async-done(((f32[512,16]{0,1:T(8,128)}), f32[512,512]{0,1:T(8,128)}) %all-gather.9.cloned.1.call-update) | async-done | bytes 1048592 | tf_op jit(solution)/shard_map/all_gather | solution.py:50
  400.6 1.6 copy.19
  403.1 11.7 %cholesky.103 = f32[128,128]{1,0:T(8,128)S(1)} custom-call(f32[128,128]{1,0:T(8,128)S(1)} %cholesky.263), custom_call_target="Cholesky" | custom-call | tf_op jit(solution)/shard_map/jit(cholesky)/cholesky | solution.py:52
  414.8 9.8 %custom-call.31 = f32[1,128,128]{1,2,0:T(8,128)S(1)} custom-call(f32[1,128,128]{2,1,0:T(8,128)S(1)} %get-tuple-element.31), custom_call_target="InvertDiagBlocksLowerTriangular" | custom-call | tf_op jit(solution)/shard_map/jit(cholesky)/cholesky | solution.py:52
  427.1 11.7 %cholesky.215 = f32[128,128]{1,0:T(8,128)S(1)} custom-call(f32[128,128]{1,0:T(8,128)S(1)} %cholesky.267), custom_call_target="Cholesky" | custom-call | tf_op jit(solution)/shard_map/jit(cholesky)/cholesky | solution.py:52
  438.8 9.9 %custom-call.32 = f32[1,128,128]{1,2,0:T(8,128)S(1)} custom-call(f32[1,128,128]{2,1,0:T(8,128)S(1)} %get-tuple-element.28), custom_call_target="InvertDiagBlocksLowerTriangular" | custom-call | tf_op jit(solution)/shard_map/jit(cholesky)/cholesky | solution.py:52
  450.9 13.2 %cholesky.236 = f32[128,128]{1,0:T(8,128)} custom-call(f32[128,128]{1,0:T(8,128)} %cholesky.272), custom_call_target="Cholesky" | custom-call | tf_op jit(solution)/shard_map/jit(cholesky)/cholesky | solution.py:52
  466.3 11.3 %custom-call.33 = f32[1,128,128]{1,2,0:T(8,128)} custom-call(f32[1,128,128]{2,1,0:T(8,128)} %get-tuple-element.25), custom_call_target="InvertDiagBlocksLowerTriangular" | custom-call | tf_op jit(solution)/shard_map/jit(cholesky)/cholesky | solution.py:52
  479.0 11.9 %cholesky.253 = f32[128,128]{1,0:T(8,128)S(1)} custom-call(f32[128,128]{1,0:T(8,128)S(1)} %convolution_subtract_fusion.6), custom_call_target="Cholesky" | custom-call | tf_op jit(solution)/shard_map/jit(cholesky)/cholesky | solution.py:52
  494.9 10.7 %while.1 = (s32[]{:T(128)}, f32[512,512]{1,0:T(8,128)S(1)}, s32[4,2]{0,1:T(2,128)S(1)}, f32[4,128,128]{2,1,0:T(8,128)}, s32[]{:T(128)}) while((s32[]{:T(128)}, f32[512,512]{1,0:T(8,128)S(1)}, s32[4,2]{0,1:T(2,128)S(1)}, f32[4,128,128]{2,1,0:T(8,128)}, s32[]{:T(128)}) %tuple.32), condition=%wide.while_cond, body=%wide.while_body.sunk | while | flops 2 | bytes 132705 | solution.py:53
  495.6 2.0 bitcast_dynamic-update-slice_fusion.2
  498.2 2.0 bitcast_dynamic-update-slice_fusion.2
  500.9 2.0 bitcast_dynamic-update-slice_fusion.2
  503.6 2.0 bitcast_dynamic-update-slice_fusion.2
  505.6 40.1 %custom-call.34 = f32[4,128,128]{1,2,0:T(8,128)S(1)} custom-call(f32[4,128,128]{2,1,0:T(8,128)} %get-tuple-element.9), custom_call_target="InvertDiagBlocksLowerTriangular" | custom-call | tf_op jit(solution)/shard_map/jit(_solve_triangular)/triangular_solve | solution.py:53
  553.2 80.1 %all-gather.11.cloned.1.call-done = f32[512,512]{0,1:T(8,128)} async-done(((f32[512,16]{0,1:T(8,128)}), f32[512,512]{0,1:T(8,128)}) %all-gather.11.cloned.1.call-update) | async-done | bytes 1048592 | tf_op jit(solution)/shard_map/all_gather | solution.py:54
  633.3 1.7 convolution_subtract_fusion.5
  (83 shorter events, 27.1 us)
Async XLA Ops:
  7.2 139.3 %all-gather.5.cloned.1.call-start = ((), (), s32[]{:S(2)}) async-start(), calls=%async_computation.1 | async-start | bytes 6488064 | tf_op jit(solution)/shard_map/all_gather | solution.py:39
  7.2 2.1 copy-start.2
  9.3 3.2 copy-start.9
  9.9 1.9 copy-start
  11.8 134.6 %copy-start.6 = (f32[3072]{0:T(1024)S(1)}, f32[3072]{0:T(1024)}, u32[]{:S(2)}) copy-start(f32[3072]{0:T(1024)} %param.9) | copy-start | bytes 36868
  11.8 134.6 %copy-start.7 = (f32[3072]{0:T(1024)S(1)}, f32[3072]{0:T(1024)}, u32[]{:S(2)}) copy-start(f32[3072]{0:T(1024)} %param.10) | copy-start | bytes 36868
  11.8 134.6 %copy-start.8 = (s32[3072]{0:T(1024)S(1)}, s32[3072]{0:T(1024)}, u32[]{:S(2)}) copy-start(s32[3072]{0:T(1024)} %param.11) | copy-start | bytes 36868
  12.5 217.7 %reduce-scatter.2.cloned.1.call-start = ((), (), s32[]{:S(2)}) async-start(), calls=%async_computation.2 | async-start | bytes 2785280 | tf_op jit(solution)/shard_map/reduce_scatter | solution.py:41
  156.0 147.6 %all-gather.7.cloned.1.call-start = ((), (), s32[]{:S(2)}) async-start(), calls=%async_computation.3 | async-start | bytes 1392640 | tf_op jit(solution)/shard_map/all_gather | solution.py:15
  231.9 168.7 %all-gather.9.cloned.1.call-start = ((), (), s32[]{:S(2)}) async-start(), calls=%async_computation.4 | async-start | bytes 1081344 | tf_op jit(solution)/shard_map/all_gather | solution.py:50
  305.3 328.0 %all-gather.11.cloned.1.call-start = ((), (), s32[]{:S(2)}) async-start(), calls=%async_computation.5 | async-start | bytes 1081344 | tf_op jit(solution)/shard_map/all_gather | solution.py:54
  400.6 1.7 copy-start.1
  426.1 119.6 %copy-start.3 = (f32[512,640]{1,0:T(8,128)S(1)}, f32[512,640]{1,0:T(8,128)}, u32[]{:S(2)}) copy-start(f32[512,640]{1,0:T(8,128)} %all-gather.7.cloned.1.call-done) | copy-start | bytes 3932164
  545.7 0.7 copy-start.4
  550.8 82.4 %copy-start.5 = (f32[2,1,16,640]{3,2,1,0:T(8,128)S(1)}, f32[2,1,16,640]{3,2,1,0:T(8,128)}, u32[]{:S(2)}) copy-start(f32[2,1,16,640]{3,2,1,0:T(8,128)} %get-tuple-element.21) | copy-start | bytes 245764
Sparse Core Ops, SparseCore 0:
  12.6 105.7 all-gather.4
  156.1 74.1 reduce-scatter.1
  232.9 70.5 all-gather.6
  307.3 93.2 all-gather.8
  553.3 79.9 all-gather.10
where the time goes:
time: 648 us; the launch traced here: 642 us
  waiting for transfers between devices  321 us (50%)
  blocking collectives  130 us (20%)
  other arithmetic  125 us (19%)
  matrix products  25.4 us (4%)
  local copies, waits for them, and re-layouts  23.3 us (4%)
  between operations  16.8 us (3%)
    psum x1, blocking collectives, shards(): products = lax.psum(partial_products, 'grow')  130 us
    all_gather x1, waiting for transfers between devices, shards(): lax.all_gather(panel_all[:, :panel_per], 'grow', axis=1, tiled=True)  94.8 us
    another operation x14, other arithmetic, shards(): lower = jnp.linalg.cholesky(shifted)  83.1 us
    all_gather x1, waiting for transfers between devices, shards(): lax.all_gather(factor_panel[:, panel_per:2 * panel_per], 'grow', axis=1,...  80.1 us
    reduce_scatter x1, waiting for transfers between devices, shards(): lax.psum_scatter(lax.dot_general(window_all, scaled, (((1,), (1,)), ((),...  74.2 us
    all_gather x1, waiting for transfers between devices, split_normal(): panel_all = lax.all_gather(own_panel, 'gcol', axis=0, tiled=True)  71.6 us
    another operation x4, other arithmetic, shards(): jax.scipy.linalg.solve_triangular(lower, panel_all, lower=True)  40.3 us
  transfers between devices with their start and end apart: 5, of which 4 were waited for; matrix products, arithmetic and copies ran while one was open for 1% of the time, Pallas kernels for 0%

commit v1 on v0

--- a/solution.py
+++ b/solution.py
@@ -32,7 +32,7 @@
     partial_products = jnp.dot(
         duals, masked, preferred_element_type=jnp.float32, precision=lax.Precision.HIGHEST
     )
-    products = lax.psum(partial_products, "grow")
+    products = jnp.sum(lax.all_gather(partial_products, "grow"), axis=0)
     reduced = costs - products
     scaling = (1 - fixed).astype(jnp.float32) * primal / jnp.sqrt(reduced * reduced + SOFTNESS)
     scaled = (masked * scaling[None, :]).astype(jnp.bfloat16)

time: 648 us -> 614 us (0.948)
  blocking collectives: 130 us -> 44.7 us
  waiting for transfers between devices: 321 us -> 372 us
    psum x1 -> x0, blocking collectives: 130 us -> none  [shards(): products = lax.psum(partial_products, 'grow')]
    all_gather x1, waiting for transfers between devices: 0.02 us -> 57.2 us  [shards(): lax.all_gather(masked[:2 * panel_per], 'grow', axis=0, tiled=True)]
    all_gather x0 -> x1, blocking collectives: none -> 44.7 us  [shards(): products = jnp.sum(lax.all_gather(partial_products, 'grow'), axis=0)]
    reduce_scatter x1, waiting for transfers between devices: 74.2 us -> 67.1 us  [shards(): lax.psum_scatter(lax.dot_general(window_all, scaled, (((1,), (1,)), ((),...]
  transfers between devices with their start and end apart: 5 -> 5, of which waited for: 4 -> 5; matrix products, arithmetic and copies ran while one was open for 1% -> 1% of each run, Pallas kernels for 0% -> 0%
where the time goes in v1:
time: 614 us; the launch traced here: 609 us
  waiting for transfers between devices  372 us (61%)
  other arithmetic  125 us (20%)
  blocking collectives  44.7 us (7%)
  matrix products  25.4 us (4%)
  local copies, waits for them, and re-layouts  23.3 us (4%)
  between operations  16.8 us (3%)
    all_gather x1, waiting for transfers between devices, shards(): lax.all_gather(panel_all[:, :panel_per], 'grow', axis=1, tiled=True)  94.8 us
    another operation x14, other arithmetic, shards(): lower = jnp.linalg.cholesky(shifted)  83.2 us
    all_gather x1, waiting for transfers between devices, shards(): lax.all_gather(factor_panel[:, panel_per:2 * panel_per], 'grow', axis=1,...  80.1 us
    all_gather x1, waiting for transfers between devices, split_normal(): panel_all = lax.all_gather(own_panel, 'gcol', axis=0, tiled=True)  72.9 us
    reduce_scatter x1, waiting for transfers between devices, shards(): lax.psum_scatter(lax.dot_general(window_all, scaled, (((1,), (1,)), ((),...  67.1 us
    all_gather x1, waiting for transfers between devices, shards(): lax.all_gather(masked[:2 * panel_per], 'grow', axis=0, tiled=True)  57.2 us
    all_gather x1, blocking collectives, shards(): products = jnp.sum(lax.all_gather(partial_products, 'grow'), axis=0)  44.7 us
    another operation x4, other arithmetic, shards(): jax.scipy.linalg.solve_triangular(lower, panel_all, lower=True)  40.3 us
  transfers between devices with their start and end apart: 5, of which 5 were waited for; matrix products, arithmetic and copies ran while one was open for 1% of the time, Pallas kernels for 0%

profile of v1, /device:TPU:1, one launch (start us, length us, event | category | flops | bytes accessed | tf_op | source)
XLA Modules:
  0.0 608.5 jit_solution(6522889724906054673)
XLA Ops:
  9.9 1.9 copy-done
  12.6 3.8 fusion.38
  16.4 44.7 %all-gather = f32[98304]{0:T(1024)S(1)} all-gather(f32[3072]{0:T(1024)S(1)} %bitcast.77), channel_id=2, replica_groups=mesh['grow'=32,'gcol'=16] {'grow'}, dimensions={0}, use_global_device_ids=true | all-gather | bytes 405504 | tf_op jit(solution)/shard_map/all_gather | solution.py:35
  61.2 57.2 %all-gather.6.cloned.1.call-done = bf16[1024,3072]{1,0:T(8,128)(2,1)} async-done(((bf16[32,3072]{1,0:T(8,128)(2,1)}), bf16[1024,3072]{1,0:T(8,128)(2,1)}) %all-gather.6.cloned.1.call-update) | async-done | bytes 6291472 | tf_op jit(solution)/shard_map/all_gather | solution.py:39
  118.4 9.5 %fusion = f32[1024,640]{1,0:T(8,128)} fusion(bf16[1024,3072]{1,0:T(8,128)(2,1)} %all-gather.6.cloned.1.call-done, bf16[640,3072]{1,0:T(8,128)(2,1)} %copy-done, f32[3072]{0:T(1024)S(1)} %rsqrt_multiply_fusion), kind=kOutput, calls=%fused_computation.3 | convolution fusion | flops 4032430080 | bytes 12857344 | tf_op jit(solution)/shard_map/dot_general | solution.py:42
  128.0 67.1 %reduce-scatter.2.cloned.1.call-done = f32[64,640]{1,0:T(8,128)} async-done(((f32[1024,640]{1,0:T(8,128)}), f32[64,640]{1,0:T(8,128)}) %reduce-scatter.2.cloned.1.call-update) | async-done | bytes 163856 | tf_op jit(solution)/shard_map/reduce_scatter | solution.py:41
  196.7 72.9 %all-gather.8.cloned.1.call-done = f32[512,640]{1,0:T(8,128)} async-done(((f32[32,640]{1,0:T(8,128)}), f32[512,640]{1,0:T(8,128)}) %all-gather.8.cloned.1.call-update) | async-done | bytes 1310736 | tf_op jit(solution)/shard_map/all_gather | solution.py:15
  271.9 94.8 %all-gather.10.cloned.1.call-done = f32[512,512]{0,1:T(8,128)} async-done(((f32[512,16]{0,1:T(8,128)}), f32[512,512]{0,1:T(8,128)}) %all-gather.10.cloned.1.call-update) | async-done | bytes 1048592 | tf_op jit(solution)/shard_map/all_gather | solution.py:50
  366.7 1.6 copy.25
  369.2 11.7 %cholesky.103 = f32[128,128]{1,0:T(8,128)S(1)} custom-call(f32[128,128]{1,0:T(8,128)S(1)} %cholesky.263), custom_call_target="Cholesky" | custom-call | tf_op jit(solution)/shard_map/jit(cholesky)/cholesky | solution.py:52
  381.0 9.8 %custom-call.31 = f32[1,128,128]{1,2,0:T(8,128)S(1)} custom-call(f32[1,128,128]{2,1,0:T(8,128)S(1)} %get-tuple-element.31), custom_call_target="InvertDiagBlocksLowerTriangular" | custom-call | tf_op jit(solution)/shard_map/jit(cholesky)/cholesky | solution.py:52
  393.2 11.7 %cholesky.215 = f32[128,128]{1,0:T(8,128)S(1)} custom-call(f32[128,128]{1,0:T(8,128)S(1)} %cholesky.267), custom_call_target="Cholesky" | custom-call | tf_op jit(solution)/shard_map/jit(cholesky)/cholesky | solution.py:52
  404.9 10.0 %custom-call.32 = f32[1,128,128]{1,2,0:T(8,128)S(1)} custom-call(f32[1,128,128]{2,1,0:T(8,128)S(1)} %get-tuple-element.28), custom_call_target="InvertDiagBlocksLowerTriangular" | custom-call | tf_op jit(solution)/shard_map/jit(cholesky)/cholesky | solution.py:52
  417.1 13.2 %cholesky.236 = f32[128,128]{1,0:T(8,128)} custom-call(f32[128,128]{1,0:T(8,128)} %cholesky.272), custom_call_target="Cholesky" | custom-call | tf_op jit(solution)/shard_map/jit(cholesky)/cholesky | solution.py:52
  432.4 11.3 %custom-call.33 = f32[1,128,128]{1,2,0:T(8,128)} custom-call(f32[1,128,128]{2,1,0:T(8,128)} %get-tuple-element.25), custom_call_target="InvertDiagBlocksLowerTriangular" | custom-call | tf_op jit(solution)/shard_map/jit(cholesky)/cholesky | solution.py:52
  445.1 11.9 %cholesky.253 = f32[128,128]{1,0:T(8,128)S(1)} custom-call(f32[128,128]{1,0:T(8,128)S(1)} %convolution_subtract_fusion.6), custom_call_target="Cholesky" | custom-call | tf_op jit(solution)/shard_map/jit(cholesky)/cholesky | solution.py:52
  461.0 10.7 %while.1 = (s32[]{:T(128)}, f32[512,512]{1,0:T(8,128)S(1)}, s32[4,2]{0,1:T(2,128)S(1)}, f32[4,128,128]{2,1,0:T(8,128)}, s32[]{:T(128)}) while((s32[]{:T(128)}, f32[512,512]{1,0:T(8,128)S(1)}, s32[4,2]{0,1:T(2,128)S(1)}, f32[4,128,128]{2,1,0:T(8,128)}, s32[]{:T(128)}) %tuple.32), condition=%wide.while_cond, body=%wide.while_body.sunk | while | flops 2 | bytes 132705 | solution.py:53
  461.7 2.0 bitcast_dynamic-update-slice_fusion.2
  464.4 2.0 bitcast_dynamic-update-slice_fusion.2
  467.0 2.0 bitcast_dynamic-update-slice_fusion.2
  469.7 2.0 bitcast_dynamic-update-slice_fusion.2
  471.7 40.1 %custom-call.34 = f32[4,128,128]{1,2,0:T(8,128)S(1)} custom-call(f32[4,128,128]{2,1,0:T(8,128)} %get-tuple-element.9), custom_call_target="InvertDiagBlocksLowerTriangular" | custom-call | tf_op jit(solution)/shard_map/jit(_solve_triangular)/triangular_solve | solution.py:53
  519.3 80.1 %all-gather.12.cloned.1.call-done = f32[512,512]{0,1:T(8,128)} async-done(((f32[512,16]{0,1:T(8,128)}), f32[512,512]{0,1:T(8,128)}) %all-gather.12.cloned.1.call-update) | async-done | bytes 1048592 | tf_op jit(solution)/shard_map/all_gather | solution.py:54
  599.4 1.7 convolution_subtract_fusion.5
  (85 shorter events, 28.8 us)
Async XLA Ops:
  7.2 111.3 %all-gather.6.cloned.1.call-start = ((), (), s32[]{:S(2)}) async-start(), calls=%async_computation.1 | async-start | bytes 6488064 | tf_op jit(solution)/shard_map/all_gather | solution.py:39
  7.2 2.1 copy-start.2
  9.3 3.2 copy-start.9
  9.9 1.9 copy-start
  12.5 182.5 %reduce-scatter.2.cloned.1.call-start = ((), (), s32[]{:S(2)}) async-start(), calls=%async_computation.2 | async-start | bytes 2785280 | tf_op jit(solution)/shard_map/reduce_scatter | solution.py:41
  12.6 48.6 %copy-start.6 = (f32[3072]{0:T(1024)S(1)}, f32[3072]{0:T(1024)}, u32[]{:S(2)}) copy-start(f32[3072]{0:T(1024)} %param.9) | copy-start | bytes 36868
  12.6 48.6 %copy-start.7 = (f32[3072]{0:T(1024)S(1)}, f32[3072]{0:T(1024)}, u32[]{:S(2)}) copy-start(f32[3072]{0:T(1024)} %param.10) | copy-start | bytes 36868
  12.6 48.6 %copy-start.8 = (s32[3072]{0:T(1024)S(1)}, s32[3072]{0:T(1024)}, u32[]{:S(2)}) copy-start(s32[3072]{0:T(1024)} %param.11) | copy-start | bytes 36868
  127.9 141.7 %all-gather.8.cloned.1.call-start = ((), (), s32[]{:S(2)}) async-start(), calls=%async_computation.3 | async-start | bytes 1392640 | tf_op jit(solution)/shard_map/all_gather | solution.py:15
  196.7 170.0 %all-gather.10.cloned.1.call-start = ((), (), s32[]{:S(2)}) async-start(), calls=%async_computation.4 | async-start | bytes 1081344 | tf_op jit(solution)/shard_map/all_gather | solution.py:50
  271.4 328.0 %all-gather.12.cloned.1.call-start = ((), (), s32[]{:S(2)}) async-start(), calls=%async_computation.5 | async-start | bytes 1081344 | tf_op jit(solution)/shard_map/all_gather | solution.py:54
  366.7 1.7 copy-start.1
  392.2 119.6 %copy-start.3 = (f32[512,640]{1,0:T(8,128)S(1)}, f32[512,640]{1,0:T(8,128)}, u32[]{:S(2)}) copy-start(f32[512,640]{1,0:T(8,128)} %all-gather.8.cloned.1.call-done) | copy-start | bytes 3932164
  511.8 0.7 copy-start.4
  517.0 82.4 %copy-start.5 = (f32[2,1,16,640]{3,2,1,0:T(8,128)S(1)}, f32[2,1,16,640]{3,2,1,0:T(8,128)}, u32[]{:S(2)}) copy-start(f32[2,1,16,640]{3,2,1,0:T(8,128)} %get-tuple-element.21) | copy-start | bytes 245764
Sparse Core Ops, SparseCore 0:
  12.6 105.7 all-gather.5
  128.0 66.9 reduce-scatter.1
  197.7 71.8 all-gather.7
  273.4 93.2 all-gather.9
  519.4 79.9 all-gather.11
